TPU v7x, 256 devices: a whole 4x4x8 slice. The times are simulated.
256 devices in a mesh: member: 16 (over x_lo, z), lat: 8 (over y, core), lon: 2 (over x_hi).
Axes of the slice: x: 4 (x_hi: 2, x_lo: 2; x = x_hi * 2 + x_lo), y: 4, z: 8, core: 2. Of those that a mesh axis runs over, the one named last changes fastest.
Arguments:
- state: float32 [32, 5, 2, 256, 1024], P('member', None, None, 'lat', 'lon'), may hold values from -4 to 4
- kick: float32 [32, 5, 2, 256, 1024], P('member', None, None, 'lat', 'lon'), may hold values from -3 to 3
- forcing: float32 [5, 2, 256, 1024], P(None, None, 'lat', 'lon'), may hold values from -4 to 4
- coupling: float32 [2, 5, 5], replicated, may hold values from -3 to 3
- clone_src: int32 [32], replicated, may hold values from 0 to 31, as said below
Outputs:
- advanced: float32 [32, 5, 2, 256, 1024], P('member', None, None, 'lat', 'lon')
Inputs may be any that keep to these rules, and one draw needn't show every extreme that they name: `clone_src`: entry m equals m for a member that is kept; a replaced member names a member that is kept.
All inputs are finite; a program needn't handle non-finite values.
Results may differ from a plain program's by a relative error of at most 0.00012.
Values sent between devices are 32-bit elements; how exact they have to be, the bound alone decides.
A program may use at most 128 MiB of HBM per device.

v0:
```python
import jax
import jax.numpy as jnp
from jax import lax
from jax.sharding import PartitionSpec as P

STEPS = 4


def with_halo(block, sides, width):
    for axis, dim in sides:
        count = lax.axis_size(axis)
        forward = [(i, i + 1) for i in range(count - 1)]
        forward.append((count - 1, 0))
        backward = [(target, source) for source, target in forward]
        low = lax.ppermute(
            lax.slice_in_dim(block, block.shape[dim] - width, None, axis=dim), axis, forward
        )
        high = lax.ppermute(lax.slice_in_dim(block, 0, width, axis=dim), axis, backward)
        block = jnp.concatenate([low, block, high], axis=dim)
    return block


def advance(padded, forcing_c, coupling):
    h = padded.shape[3] - 4
    w = padded.shape[4] - 4

    def part(di, dj):
        return padded[:, :, :, 2 + di : 2 + di + h, 2 + dj : 2 + dj + w]

    centre = part(0, 0)
    along_x = (8.0 * (part(0, 1) - part(0, -1)) - (part(0, 2) - part(0, -2))) / 12.0
    along_y = (8.0 * (part(1, 0) - part(-1, 0)) - (part(2, 0) - part(-2, 0))) / 12.0
    near = part(0, 1) + part(0, -1) + part(1, 0) + part(-1, 0)
    far_sum = part(0, 2) + part(0, -2) + part(2, 0) + part(-2, 0)
    laplace = (16.0 * near - far_sum - 60.0 * centre) / 12.0
    wind_u = centre[:, 0:1]
    wind_v = centre[:, 1:2]
    mixed = jnp.einsum("kvw,mwkij->mvkij", coupling, centre, precision=lax.Precision.HIGHEST)
    return centre + (
        -0.05 * (wind_u * along_x + wind_v * along_y)
        + 0.05 * laplace
        + 0.25 * mixed
        + 0.1 * forcing_c
    )


def shards(state, kick, forcing, coupling, clone_src):
    per_dev = state.shape[0]
    group = lax.axis_index("member")
    sources = lax.dynamic_slice_in_dim(clone_src, group * per_dev, per_dev)
    piece = lax.all_gather(state, "member", axis=0, tiled=True)
    count = piece.shape[0]
    inside = (sources >= 0) & (sources < count)
    rows = jnp.take(piece, jnp.clip(sources, 0, count - 1), axis=0)
    field = jnp.where(inside[:, None, None, None, None], rows, jnp.zeros_like(state))
    field = field + kick
    lat_dev = state.shape[3]
    lat_total = lat_dev * lax.axis_size("lat")
    base = lax.axis_index("lat") * lat_dev

    def zero_rows(values, first_row):
        rows = first_row + jnp.arange(values.shape[3], dtype=jnp.int32)
        keep = (rows >= 0) & (rows < lat_total)
        return jnp.where(keep[:, None], values, 0.0)

    for step in range(STEPS):
        padded = with_halo(field, (("lat", 3), ("lon", 4)), 2)
        padded = zero_rows(padded, base - 2)
        field = advance(padded, forcing, coupling)
    return field


def solution(mesh):
    in_specs = (
        P("member", None, None, "lat", "lon"),
        P("member", None, None, "lat", "lon"),
        P(None, None, "lat", "lon"),
        P(),
        P(),
    )
    out_specs = P("member", None, None, "lat", "lon")
    return jax.shard_map(shards, mesh=mesh, in_specs=in_specs, out_specs=out_specs, check_vma=False)
```

profile of v0, /device:TPU:1, one launch (start us, length us, event | category | flops | bytes accessed | tf_op | source)
XLA Modules:
  0.0 354.2 jit_solution(12120643734006682233)
XLA Ops:
  8.0 232.1 %all-gather.2.cloned.1.call-done = f32[32,5,2,32,512]{4,3,2,1,0:T(8,128)} async-done(((f32[2,5,2,32,512]{4,3,2,1,0:T(8,128)}), f32[32,5,2,32,512]{4,3,2,1,0:T(8,128)}) %all-gather.2.cloned.1.call-update) | async-done | bytes 20971536 | tf_op jit(solution)/shard_map/all_gather | solution.py:51
  240.1 7.6 %gather_fusion = f32[2,5,2,32,512]{4,3,2,1,0:T(8,128)S(1)} fusion(f32[32,5,2,32,512]{4,3,2,1,0:T(8,128)} %all-gather.2.cloned.1.call-done, s32[1024]{0:T(1024)S(1)} %pad_clamp_fusion), kind=kCustom, calls=%fused_computation | custom fusion | bytes 2621448 | tf_op jit(solution)/shard_map/jit(_take)/gather | solution.py:54
  247.7 3.9 %copy_add_fusion = f32[2,5,2,32,512]{4,1,3,0,2:T(8,128)S(1)} fusion(f32[2,5,2,32,512]{4,3,2,1,0:T(8,128)} %param.6, f32[2,5,2,32,512]{4,3,2,1,0:T(8,128)S(1)} %gather_fusion, pred[2]{0:T(512)(128)(4,1)S(1)} %get-tuple-element.5, pred[2]{0:T(512)(128)(4,1)S(1)} %get-tuple-element.31), kind=kLoop, calls=%fused_computation.17 | loop fusion | flops 983040 | bytes 3932164 | tf_op jit(solution)/shard_map/add | solution.py:56
  251.6 1.9 collective-permute-start
  253.6 1.9 collective-permute-done
  255.5 2.5 collective-permute-done.1
  258.1 1.8 pad_maximum_fusion.11
  261.4 2.5 collective-permute-start.3
  265.8 2.2 collective-permute-done.2
  268.8 1.9 maximum_select_fusion
  271.9 6.2 %fusion.7 = f32[2,5,2,32,512]{4,1,3,0,2:T(8,128)S(1)} fusion(f32[2,5,2,36,516]{4,1,3,0,2:T(8,128)S(1)} %maximum_select_fusion, f32[5,2,32,512]{3,0,2,1:T(8,128)S(1)} %copy-done.1, f32[2,2,32,512]{3,2,0,1:T(8,128)S(1)} %get-tuple-element.32, f32[2,2,32,512]{3,2,0,1:T(8,128)S(1)} %get-tuple-element.33, f32[2,5,5,1,1]{2,0,1,4,3:T(2,128)S(1)} %bitcast.50), kind=kOutput, calls=%fused_computation.16 | convolution fusion | flops 28835840 | bytes 23860224 | tf_op jit(solution)/shard_map/kvw,mwkij->mvkij/dot_general | solution.py:38
  279.7 1.8 collective-permute-done.4
  281.5 2.7 collective-permute-done.5
  286.2 2.6 collective-permute-start.7
  294.1 6.2 %fusion.5 = f32[2,5,2,32,512]{4,1,3,0,2:T(8,128)S(1)} fusion(f32[2,5,2,36,516]{4,1,3,0,2:T(8,128)S(1)} %maximum_select_fusion.1, f32[2,2,32,512]{3,2,0,1:T(8,128)S(1)} %bitcast.58, f32[2,2,32,512]{3,2,0,1:T(8,128)S(1)} %bitcast.55, f32[5,2,32,512]{3,0,2,1:T(8,128)S(1)} %copy-done.2, f32[2,5,5,1,1]{2,0,1,4,3:T(2,128)S(1)} %bitcast.53), kind=kOutput, calls=%fused_computation.13 | convolution fusion | flops 28835840 | bytes 23860224 | tf_op jit(solution)/shard_map/kvw,mwkij->mvkij/dot_general | solution.py:38
  303.6 2.3 collective-permute-done.9
  307.0 2.3 collective-permute-start.10
  311.7 2.2 collective-permute-done.11
  317.2 6.2 %fusion.3 = f32[2,5,2,32,512]{4,1,3,0,2:T(8,128)S(1)} fusion(f32[2,5,2,36,516]{4,1,3,0,2:T(8,128)S(1)} %maximum_select_fusion.2, f32[2,2,32,512]{3,2,0,1:T(8,128)S(1)} %bitcast.59, f32[2,2,32,512]{3,2,0,1:T(8,128)S(1)} %bitcast.56, f32[5,2,32,512]{3,0,2,1:T(8,128)S(1)} %copy-done.3, f32[2,5,5,1,1]{2,0,1,4,3:T(2,128)S(1)} %bitcast.52), kind=kOutput, calls=%fused_computation.10 | convolution fusion | flops 28835840 | bytes 23860224 | tf_op jit(solution)/shard_map/kvw,mwkij->mvkij/dot_general | solution.py:38
  323.5 1.4 collective-permute-start.12
  325.0 2.6 collective-permute-start.13
  331.4 2.6 collective-permute-start.15
  339.3 6.2 %fusion.1 = f32[2,5,2,32,512]{4,1,3,0,2:T(8,128)S(1)} fusion(f32[2,5,2,36,516]{4,1,3,0,2:T(8,128)S(1)} %maximum_select_fusion.3, f32[2,2,32,512]{3,2,0,1:T(8,128)S(1)} %bitcast.57, f32[2,2,32,512]{3,2,0,1:T(8,128)S(1)} %bitcast.54, f32[5,2,32,512]{3,0,2,1:T(8,128)S(1)} %copy-done.4, f32[2,5,5,1,1]{2,0,1,4,3:T(2,128)S(1)} %bitcast.51), kind=kOutput, calls=%fused_computation.7 | convolution fusion | flops 28835840 | bytes 23860224 | tf_op jit(solution)/shard_map/kvw,mwkij->mvkij/dot_general | solution.py:38
  345.5 1.8 copy.44
  (74 shorter events, 34.9 us)
Async XLA Ops:
  6.5 265.4 %copy-start = (f32[2,5,5]{2,0,1:T(2,128)S(1)}, f32[2,5,5]{2,0,1:T(2,128)}, u32[]{:S(2)}) copy-start(f32[2,5,5]{2,0,1:T(2,128)} %param.8) | copy-start | bytes 604
  6.5 233.6 %all-gather.2.cloned.1.call-start = ((), (), s32[]{:S(2)}) async-start(), calls=%async_computation | async-start | bytes 22282240 | tf_op jit(solution)/shard_map/all_gather | solution.py:51
  247.7 5.9 %copy-start.5 = (f32[5,2,32,512]{3,2,1,0:T(8,128)S(1)}, f32[5,2,32,512]{3,2,1,0:T(8,128)}, u32[]{:S(2)}) copy-start(f32[5,2,32,512]{3,2,1,0:T(8,128)} %param.7) | copy-start | bytes 1966084
  251.6 3.9 %collective-permute-start = (f32[2,5,2,2,512]{4,1,3,0,2:T(8,128)S(1)}, f32[2,5,2,2,512]{4,1,3,0,2:T(8,128)S(1)}, u32[]{:S(2)}, u32[]{:S(2)}) collective-permute-start(f32[2,5,2,2,512]{4,1,3,0,2:T(8,128)S(1)} %get-tuple-element.29), channel_id=1, source_target_pairs={{0,2},{2,4},{4,6},{6,8},{8,10},{10,12},{12,14},{14,0},{1,3},{3,5},... | collective-permute-start | bytes 245768 | tf_op jit(solution)/shard_map/ppermute | solution.py:15
  253.6 4.5 %collective-permute-start.1 = (f32[2,5,2,2,512]{4,1,3,0,2:T(8,128)S(1)}, f32[2,5,2,2,512]{4,1,3,0,2:T(8,128)}, u32[]{:S(2)}, u32[]{:S(2)}) collective-permute-start(f32[2,5,2,2,512]{4,1,3,0,2:T(8,128)S(1)} %get-tuple-element.30), channel_id=1, source_target_pairs={{2,0},{4,2},{6,4},{8,6},{10,8},{12,10},{14,12},{0,14},{3,1},{5,3},... | collective-permute-start | bytes 245768 | tf_op jit(solution)/shard_map/ppermute | solution.py:18
  261.4 7.0 %collective-permute-start.3 = (f32[2,5,2,36,2]{3,4,2,1,0:T(2,128)S(1)}, f32[2,5,2,36,2]{3,4,2,1,0:T(2,128)S(1)}, u32[]{:S(2)}, u32[]{:S(2)}) collective-permute-start(f32[2,5,2,36,2]{3,4,2,1,0:T(2,128)S(1)} %copy.24), channel_id=1, source_target_pairs={{1,0},{0,1},{3,2},{2,3},{5,4},{4,5},{7,6},{6,7},{9,8},{8,9},{11,10... | collective-permute-start | bytes 17288 | tf_op jit(solution)/shard_map/ppermute | solution.py:18
  263.9 4.1 %collective-permute-start.2 = (f32[2,5,2,36,2]{3,4,2,1,0:T(2,128)S(1)}, f32[2,5,2,36,2]{3,4,2,1,0:T(2,128)S(1)}, u32[]{:S(2)}, u32[]{:S(2)}) collective-permute-start(f32[2,5,2,36,2]{3,4,2,1,0:T(2,128)S(1)} %copy.23), channel_id=1, source_target_pairs={{0,1},{1,0},{2,3},{3,2},{4,5},{5,4},{6,7},{7,6},{8,9},{9,8},{10,11... | collective-permute-start | bytes 17288 | tf_op jit(solution)/shard_map/ppermute | solution.py:15
  270.7 1.2 copy-start.1
  278.2 3.3 collective-permute-start.4
  279.5 4.7 %collective-permute-start.5 = (f32[2,5,2,2,512]{4,1,3,0,2:T(8,128)S(1)}, f32[2,5,2,2,512]{4,1,3,0,2:T(8,128)S(1)}, u32[]{:S(2)}, u32[]{:S(2)}) collective-permute-start(f32[2,5,2,2,512]{4,1,3,0,2:T(8,128)S(1)} %get-tuple-element.28), channel_id=1, source_target_pairs={{2,0},{4,2},{6,4},{8,6},{10,8},{12,10},{14,12},{0,14},{3,1},{5,3},... | collective-permute-start | bytes 245768 | tf_op jit(solution)/shard_map/ppermute | solution.py:18
  285.3 4.3 %collective-permute-start.6 = (f32[2,5,2,36,2]{3,4,2,1,0:T(2,128)}, f32[2,5,2,36,2]{3,4,2,1,0:T(2,128)S(1)}, u32[]{:S(2)}, u32[]{:S(2)}) collective-permute-start(f32[2,5,2,36,2]{3,4,2,1,0:T(2,128)} %copy.29), channel_id=1, source_target_pairs={{0,1},{1,0},{2,3},{3,2},{4,5},{5,4},{6,7},{7,6},{8,9},{9,8},{10,11... | collective-permute-start | bytes 17288 | tf_op jit(solution)/shard_map/ppermute | solution.py:15
  286.2 4.5 %collective-permute-start.7 = (f32[2,5,2,36,2]{3,4,2,1,0:T(2,128)S(1)}, f32[2,5,2,36,2]{3,4,2,1,0:T(2,128)}, u32[]{:S(2)}, u32[]{:S(2)}) collective-permute-start(f32[2,5,2,36,2]{3,4,2,1,0:T(2,128)S(1)} %copy.30), channel_id=1, source_target_pairs={{1,0},{0,1},{3,2},{2,3},{5,4},{4,5},{7,6},{6,7},{9,8},{8,9},{11,10... | collective-permute-start | bytes 17288 | tf_op jit(solution)/shard_map/ppermute | solution.py:18
  292.9 1.2 copy-start.2
  300.4 3.2 collective-permute-start.8
  301.5 4.4 %collective-permute-start.9 = (f32[2,5,2,2,512]{4,1,3,0,2:T(8,128)S(1)}, f32[2,5,2,2,512]{4,1,3,0,2:T(8,128)S(1)}, u32[]{:S(2)}, u32[]{:S(2)}) collective-permute-start(f32[2,5,2,2,512]{4,1,3,0,2:T(8,128)S(1)} %get-tuple-element.26), channel_id=1, source_target_pairs={{2,0},{4,2},{6,4},{8,6},{10,8},{12,10},{14,12},{0,14},{3,1},{5,3},... | collective-permute-start | bytes 245768 | tf_op jit(solution)/shard_map/ppermute | solution.py:18
  307.0 4.3 %collective-permute-start.10 = (f32[2,5,2,36,2]{3,4,2,1,0:T(2,128)}, f32[2,5,2,36,2]{3,4,2,1,0:T(2,128)S(1)}, u32[]{:S(2)}, u32[]{:S(2)}) collective-permute-start(f32[2,5,2,36,2]{3,4,2,1,0:T(2,128)} %copy.34), channel_id=1, source_target_pairs={{0,1},{1,0},{2,3},{3,2},{4,5},{5,4},{6,7},{7,6},{8,9},{9,8},{10,11... | collective-permute-start | bytes 17288 | tf_op jit(solution)/shard_map/ppermute | solution.py:15
  309.5 4.3 %collective-permute-start.11 = (f32[2,5,2,36,2]{3,4,2,1,0:T(2,128)S(1)}, f32[2,5,2,36,2]{3,4,2,1,0:T(2,128)}, u32[]{:S(2)}, u32[]{:S(2)}) collective-permute-start(f32[2,5,2,36,2]{3,4,2,1,0:T(2,128)S(1)} %copy.35), channel_id=1, source_target_pairs={{1,0},{0,1},{3,2},{2,3},{5,4},{4,5},{7,6},{6,7},{9,8},{8,9},{11,10... | collective-permute-start | bytes 17288 | tf_op jit(solution)/shard_map/ppermute | solution.py:18
  316.0 1.2 copy-start.3
  323.5 4.8 %collective-permute-start.12 = (f32[2,5,2,2,512]{4,1,3,0,2:T(8,128)S(1)}, f32[2,5,2,2,512]{4,1,3,0,2:T(8,128)S(1)}, u32[]{:S(2)}, u32[]{:S(2)}) collective-permute-start(f32[2,5,2,2,512]{4,1,3,0,2:T(8,128)S(1)} %get-tuple-element.23), channel_id=1, source_target_pairs={{0,2},{2,4},{4,6},{6,8},{8,10},{10,12},{12,14},{14,0},{1,3},{3,5},... | collective-permute-start | bytes 245768 | tf_op jit(solution)/shard_map/ppermute | solution.py:15
  325.0 4.4 %collective-permute-start.13 = (f32[2,5,2,2,512]{4,1,3,0,2:T(8,128)S(1)}, f32[2,5,2,2,512]{4,1,3,0,2:T(8,128)S(1)}, u32[]{:S(2)}, u32[]{:S(2)}) collective-permute-start(f32[2,5,2,2,512]{4,1,3,0,2:T(8,128)S(1)} %get-tuple-element.24), channel_id=1, source_target_pairs={{2,0},{4,2},{6,4},{8,6},{10,8},{12,10},{14,12},{0,14},{3,1},{5,3},... | collective-permute-start | bytes 245768 | tf_op jit(solution)/shard_map/ppermute | solution.py:18
  330.4 4.3 %collective-permute-start.14 = (f32[2,5,2,36,2]{3,4,2,1,0:T(2,128)}, f32[2,5,2,36,2]{3,4,2,1,0:T(2,128)S(1)}, u32[]{:S(2)}, u32[]{:S(2)}) collective-permute-start(f32[2,5,2,36,2]{3,4,2,1,0:T(2,128)} %copy.39), channel_id=1, source_target_pairs={{0,1},{1,0},{2,3},{3,2},{4,5},{5,4},{6,7},{7,6},{8,9},{9,8},{10,11... | collective-permute-start | bytes 17288 | tf_op jit(solution)/shard_map/ppermute | solution.py:15
  331.4 4.5 %collective-permute-start.15 = (f32[2,5,2,36,2]{3,4,2,1,0:T(2,128)S(1)}, f32[2,5,2,36,2]{3,4,2,1,0:T(2,128)}, u32[]{:S(2)}, u32[]{:S(2)}) collective-permute-start(f32[2,5,2,36,2]{3,4,2,1,0:T(2,128)S(1)} %copy.40), channel_id=1, source_target_pairs={{1,0},{0,1},{3,2},{2,3},{5,4},{4,5},{7,6},{6,7},{9,8},{8,9},{11,10... | collective-permute-start | bytes 17288 | tf_op jit(solution)/shard_map/ppermute | solution.py:18
  338.1 1.2 copy-start.4
Sparse Core Ops, SparseCore 0:
  9.1 230.9 all-gather.1
where the time goes:
time: 358 us; the launch traced here: 354 us
  waiting for transfers between devices  255 us (71%)
  matrix products  24.9 us (7%)
  starting transfers between devices  22.4 us (6%)
  local copies, waits for them, and re-layouts  20.8 us (6%)
  other arithmetic  16.9 us (5%)
  between operations  13.7 us (4%)
    all_gather x1, waiting for transfers between devices, shards(): piece = lax.all_gather(state, 'member', axis=0, tiled=True)  232 us
    dot_general x4, matrix products, advance(): jnp.einsum('kvw,mwkij->mvkij', coupling, centre, precision=lax.Precision....  24.9 us
    ppermute x8, waiting for transfers between devices, with_halo(): lax.ppermute(lax.slice_in_dim(block, 0, width, axis=dim), axis, backward)  12.3 us
    ppermute x8, starting transfers between devices, with_halo(): lax.ppermute(lax.slice_in_dim(block, 0, width, axis=dim), axis, backward)  12.3 us
    ppermute x8, waiting for transfers between devices, with_halo(): lax.ppermute(lax.slice_in_dim(block, block.shape[dim] - width, None, axis...  10.2 us
    ppermute x8, starting transfers between devices, with_halo(): lax.ppermute(lax.slice_in_dim(block, block.shape[dim] - width, None, axis...  10.1 us
    gather x1, local copies, waits for them, and re-layouts, shards(): rows = jnp.take(piece, jnp.clip(sources, 0, count - 1), axis=0)  7.59 us
  transfers between devices with their start and end apart: 17, of which 16 were waited for; matrix products, arithmetic and copies ran while one was open for 1% of the time, Pallas kernels for 0%

commit v1 on v0

v1 whole, which is shorter than its diff:
```python
import functools

import jax
import jax.numpy as jnp
from jax import lax
from jax.experimental import pallas as pl
from jax.experimental.pallas import tpu as pltpu
from jax.sharding import PartitionSpec as P

STEPS = 4
HALO = 8
MESH = pl.DeviceIdType.MESH


def roll(values, shift):
    return pltpu.roll(values, shift % values.shape[-1], axis=values.ndim - 1)


def exchange_kernel(
    chunks, clone, state, kick, forcing, e_ref, f_ref,
    comb, outgoing, pack, packf, landed, landedf,
    load_sem, send1, recv1, send2, recv2, own_sem, edge_send, edge_recv, *pools,
):
    n = lax.axis_size("member")
    nlat = lax.axis_size("lat")
    me = lax.axis_index("member")
    lat = lax.axis_index("lat")
    lon = lax.axis_index("lon")
    planes = state.shape[1]
    per_chunk = planes // chunks
    up = lax.rem(lat + nlat - 1, nlat)
    down = lax.rem(lat + 1, nlat)
    across = 1 - lon

    load = pltpu.make_async_copy(state, comb.at[0:2], load_sem)
    load.start()

    barrier = pltpu.get_barrier_semaphore()

    def greet(r, _):
        pl.semaphore_signal(barrier, 1, device_id={"member": lax.rem(me + r, n)}, device_id_type=MESH)
        return 0

    lax.fori_loop(1, n, greet, 0)
    for peer in (
        {"lat": up}, {"lat": down}, {"lon": across},
        {"lat": up, "lon": across}, {"lat": down, "lon": across},
    ):
        pl.semaphore_signal(barrier, 1, device_id=peer, device_id_type=MESH)
    load.wait()
    pl.semaphore_wait(barrier, n - 1 + 5)

    def window(piece):
        rows = pl.ds(pl.multiple_of(piece // 4 * 8, 8), 8)
        cols = pl.ds(pl.multiple_of(lax.rem(piece, 4) * 128, 128), 128)
        return rows, cols

    def spread(k, r):
        peer = lax.rem(me + r, n)
        rows, cols = window(peer)
        some = pl.ds(k * per_chunk, per_chunk)
        return pltpu.make_async_remote_copy(
            comb.at[0:2, some, rows, cols], pools[k].at[me],
            send1.at[k, r], recv1.at[k, r], device_id={"member": peer}, device_id_type=MESH,
        )

    def collect(k, r):
        peer = lax.rem(me + r, n)
        rows, cols = window(me)
        some = pl.ds(k * per_chunk, per_chunk)
        return pltpu.make_async_remote_copy(
            outgoing.at[peer, :, some], comb.at[2:4, some, rows, cols],
            send2.at[k, r], recv2.at[k, r], device_id={"member": peer}, device_id_type=MESH,
        )

    for k in range(chunks):
        lax.fori_loop(1, n, lambda r, c: (spread(k, r).start(), c)[1], 0)
    my_rows, my_cols = window(me)
    owns = [
        pltpu.make_async_copy(
            comb.at[0:2, k * per_chunk : (k + 1) * per_chunk, my_rows, my_cols], pools[k].at[me], own_sem.at[k]
        )
        for k in range(chunks)
    ]
    for own in owns:
        own.start()

    lane = lax.broadcasted_iota(jnp.int32, (32, 128), 1)

    def edge_copies(rim, packed, arrived, base):
        hops = (
            (rim.at[:, 0:4, 8:16], rim.at[:, 0:4, 40:48], {"lat": up}),
            (rim.at[:, 0:4, 32:40], rim.at[:, 0:4, 0:8], {"lat": down}),
            (packed, arrived.at[:, 8:40], {"lon": across}),
            (packed.at[:, 0:8], arrived.at[:, 40:48], {"lat": up, "lon": across}),
            (packed.at[:, 24:32], arrived.at[:, 0:8], {"lat": down, "lon": across}),
        )
        return [
            pltpu.make_async_remote_copy(
                source, target, edge_send.at[base + i], edge_recv.at[base + i],
                device_id=peer, device_id_type=MESH,
            )
            for i, (source, target, peer) in enumerate(hops)
        ]

    def pack_edges(rim, packed, count):
        for group in range((count + 7) // 8):
            total = None
            for slot in range(min(8, count - 8 * group)):
                p = 8 * group + slot
                tile = jnp.where(lane < 64, rim[p, 0, 8:40], rim[p, 3, 8:40])
                tile = roll(tile, 16 * slot)
                if total is None:
                    total = tile
                else:
                    first = 16 * slot - 8
                    total = jnp.where((lane >= first) & (lane < first + 16), tile, total)
            packed[group] = total

    def unpack_edges(rim, arrived, count):
        for p in range(count):
            rim[p, 4] = roll(arrived[p // 8], -16 * (p % 8))

    def clear_outside(rim):
        @pl.when(lat == 0)
        def _():
            rim[:, :, 0:8] = jnp.zeros((rim.shape[0], 5, 8, 128), jnp.float32)

        @pl.when(lat == nlat - 1)
        def _():
            rim[:, :, 40:48] = jnp.zeros((rim.shape[0], 5, 8, 128), jnp.float32)

    for ct in range(4):
        f_ref[:, ct, 8:40] = forcing[:, :, ct * 128 : ct * 128 + 128]
    pack_edges(f_ref, packf, planes)
    f_copies = edge_copies(f_ref, packf, landedf, 5)
    for copy in f_copies:
        copy.start()

    for k in range(chunks):
        owns[k].wait()
        lax.fori_loop(1, n, lambda r, c: (spread(k, r).wait_recv(), c)[1], 0)
        some = pl.ds(k * per_chunk, per_chunk)

        def choose(d, c):
            for j in range(2):
                source = clone[2 * d + j]
                outgoing[d, j, some] = pools[k][source // 2, lax.rem(source, 2)]
            return c

        lax.fori_loop(0, n, choose, 0)
        lax.fori_loop(1, n, lambda r, c: (collect(k, r).start(), c)[1], 0)
    mine = pltpu.make_async_copy(outgoing.at[me], comb.at[2:4, :, my_rows, my_cols], own_sem.at[0])
    mine.start()
    for k in range(chunks):
        lax.fori_loop(1, n, lambda r, c: (spread(k, r).wait_send(), c)[1], 0)
    mine.wait()
    for k in range(chunks):
        lax.fori_loop(1, n, lambda r, c: (collect(k, r).wait_recv(), c)[1], 0)

    def begin(p, c):
        for j in range(2):
            source = clone[2 * me + j]
            pick = jnp.where(source // 2 == me, lax.rem(source, 2), 2 + j)
            for ct in range(4):
                cols = slice(ct * 128, ct * 128 + 128)
                e_ref[j * planes + p, ct, 8:40] = comb[pick, p, :, cols] + kick[j, p, :, cols]
        return c

    lax.fori_loop(0, planes, begin, 0)
    pack_edges(e_ref, pack, 2 * planes)
    e_copies = edge_copies(e_ref, pack, landed, 0)
    for copy in e_copies:
        copy.start()
    for copy in f_copies:
        copy.wait()
    unpack_edges(f_ref, landedf, planes)
    for k in range(chunks):
        lax.fori_loop(1, n, lambda r, c: (collect(k, r).wait_send(), c)[1], 0)
    for copy in e_copies:
        copy.wait()
    unpack_edges(e_ref, landed, 2 * planes)
    clear_outside(e_ref)


def step_kernel(coupling, edge, e_ref, f_ref, out_ref, work_a, work_b, mix):
    for k in range(2):
        for v in range(5):
            for w in range(5):
                scaled = 0.25 * coupling[k, v, w]
                mix[k, v, w] = scaled + 0.75 if v == w else scaled
    lane = lax.broadcasted_iota(jnp.int32, (8, 128), 1)
    row_at = lax.broadcasted_iota(jnp.int32, (8, 128), 0)
    low, high = edge[0], edge[1]
    one12 = 1.0 / 12.0

    def sweep(source, target, starts, last):
        tiles = 4 if last else 5

        def block(combo, row):
            m, k = combo // 2, lax.rem(combo, 2)
            base = m * 10 + k
            centre = [[source[base + 2 * v, c, pl.ds(row, 8)] for c in range(5)] for v in range(5)]
            for c in range(tiles):
                u = centre[0][c]
                w = centre[1][c]
                u8, u1 = u * (-0.4 * one12), u * (0.05 * one12)
                v8, v1 = w * (-0.4 * one12), w * (0.05 * one12)
                for v in range(5):
                    here = centre[v]
                    before, after = here[(c + 4) % 5], here[(c + 1) % 5]
                    w1 = jnp.where(lane < 1, roll(before, 1), roll(here[c], 1))
                    w2 = jnp.where(lane < 2, roll(before, 2), roll(here[c], 2))
                    e1 = jnp.where(lane >= 127, roll(after, -1), roll(here[c], -1))
                    e2 = jnp.where(lane >= 126, roll(after, -2), roll(here[c], -2))
                    p = base + 2 * v
                    n1 = source[p, c, pl.ds(row - 1, 8)]
                    n2 = source[p, c, pl.ds(row - 2, 8)]
                    s1 = source[p, c, pl.ds(row + 1, 8)]
                    s2 = source[p, c, pl.ds(row + 2, 8)]
                    near = (e1 + w1) + (s1 + n1)
                    far = (e2 + w2) + (s2 + n2)
                    total = u8 * (e1 - w1) + u1 * (e2 - w2) + v8 * (s1 - n1) + v1 * (s2 - n2)
                    total = total + (near * (0.8 * one12) - far * (0.05 * one12))
                    total = total + 0.1 * f_ref[2 * v + k, c, pl.ds(row, 8)]
                    for q in range(5):
                        total = total + mix[k, v, q] * centre[q][c]
                    if last:
                        out_ref[m, 2 * v + k, pl.ds(row - HALO, 8), c * 128 : c * 128 + 128] = total
                    else:
                        inside = (row_at + row >= low) & (row_at + row < high)
                        target[p, c, pl.ds(row, 8)] = jnp.where(inside, total, 0.0)

        def combos(combo, _):
            for row in starts:
                block(combo, row)
            return 0

        lax.fori_loop(0, 4, combos, 0)

    sweep(e_ref, work_a, (2, 10, 18, 26, 34, 38), False)
    sweep(work_a, work_b, (4, 12, 20, 28, 36), False)
    sweep(work_b, work_a, (6, 14, 22, 30, 34), False)
    sweep(work_a, None, (8, 16, 24, 32), True)


def shards(state, kick, forcing, coupling, clone_src):
    shape = state.shape
    planes = shape[1] * shape[2]
    flat = (shape[0], planes, shape[3], shape[4])
    n = lax.axis_size("member")
    chunks = 2
    f32 = jnp.float32
    vmem = pl.BlockSpec(memory_space=pltpu.VMEM)
    smem = pl.BlockSpec(memory_space=pltpu.SMEM)
    dma = pltpu.SemaphoreType.DMA
    e, f = pl.pallas_call(
        functools.partial(exchange_kernel, chunks),
        out_shape=(
            jax.ShapeDtypeStruct((2 * planes, 5, 48, 128), f32),
            jax.ShapeDtypeStruct((planes, 5, 48, 128), f32),
        ),
        in_specs=[smem, pl.BlockSpec(memory_space=pl.ANY), vmem, vmem],
        out_specs=(vmem, vmem),
        scratch_shapes=[
            pltpu.VMEM((4,) + flat[1:], f32),
            pltpu.VMEM((n, 2, planes, 8, 128), f32),
            pltpu.VMEM((3, 32, 128), f32),
            pltpu.VMEM((2, 32, 128), f32),
            pltpu.VMEM((3, 48, 128), f32),
            pltpu.VMEM((2, 48, 128), f32),
            dma(()),
            dma((chunks, n)), dma((chunks, n)), dma((chunks, n)), dma((chunks, n)),
            dma((chunks,)), dma((10,)), dma((10,)),
        ]
        + [pltpu.VMEM((n, 2, planes // chunks, 8, 128), f32)] * chunks,
        compiler_params=pltpu.CompilerParams(collective_id=0, has_side_effects=True),
        name="exchange",
    )(clone_src, state.reshape(flat), kick.reshape(flat), forcing.reshape(flat[1:]))
    lat, nlat = lax.axis_index("lat"), lax.axis_size("lat")
    edge = jnp.stack([jnp.where(lat == 0, HALO, 0), jnp.where(lat == nlat - 1, 40, 48)]).astype(jnp.int32)
    out = pl.pallas_call(
        step_kernel,
        out_shape=jax.ShapeDtypeStruct(flat, f32),
        in_specs=[smem, smem, vmem, vmem],
        out_specs=vmem,
        scratch_shapes=[
            pltpu.VMEM((2 * planes, 5, 48, 128), f32),
            pltpu.VMEM((2 * planes, 5, 48, 128), f32),
            pltpu.SMEM((2, 5, 5), f32),
        ],
        name="steps",
    )(coupling, edge, e, f)
    return out.reshape(shape)


def solution(mesh):
    block = P("member", None, None, "lat", "lon")
    in_specs = (block, block, P(None, None, "lat", "lon"), P(), P())
    return jax.shard_map(shards, mesh=mesh, in_specs=in_specs, out_specs=block, check_vma=False)
```

time: 358 us -> 98.8 us (0.28); the launches traced: 354 us -> 98.6 us
  waiting for transfers between devices: 255 us -> 0 us
  Pallas kernels: 0 us -> 96.7 us
  matrix products: 24.9 us -> 0 us
  starting transfers between devices: 22.4 us -> 0 us
  local copies, waits for them, and re-layouts: 20.8 us -> 1.29 us
  other arithmetic: 16.9 us -> 0.59 us
  between operations: 13.7 us -> 0.01 us
    all_gather x1 -> x0, waiting for transfers between devices: 232 us -> none  [shards(): piece = lax.all_gather(state, 'member', axis=0, tiled=True)]
    pallas_call x0 -> x2, Pallas kernels: none -> 96.7 us  [the longest x1 79.5 us: shards(): pl.pallas_call(functools.partial(exchange_kernel, chunks), out_shape=(jax...]
    dot_general x4 -> x0, matrix products: 24.9 us -> none  [advance(): jnp.einsum('kvw,mwkij->mvkij', coupling, centre, precision=lax.Precision....]
    ppermute x16 -> x0, waiting for transfers between devices: 22.6 us -> none  [the longest x8 12.3 us: with_halo(): lax.ppermute(lax.slice_in_dim(block, 0, width, axis=dim), axis, backward)]
    ppermute x16 -> x0, starting transfers between devices: 22.4 us -> none  [the longest x8 12.3 us: with_halo(): lax.ppermute(lax.slice_in_dim(block, 0, width, axis=dim), axis, backward)]
    gather x1 -> x0, local copies, waits for them, and re-layouts: 7.59 us -> none  [shards(): rows = jnp.take(piece, jnp.clip(sources, 0, count - 1), axis=0)]
    select_n x4 -> x0, other arithmetic: 5.13 us -> none  [zero_rows(): return jnp.where(keep[:, None], values, 0.0)]
    ppermute x8 -> x0, local copies, waits for them, and re-layouts: 4.95 us -> none  [the longest x4 3.54 us: with_halo(): lax.ppermute(lax.slice_in_dim(block, 0, width, axis=dim), axis, backward)]
  transfers between devices with their start and end apart: 17 -> 0, of which waited for: 16 -> 0; matrix products, arithmetic and copies ran while one was open for 1% -> 0% of each run, Pallas kernels for 0% -> 0%
where the time goes in v1:
time: 98.8 us; the launch traced here: 98.6 us
  Pallas kernels  96.7 us (98%)
  local copies, waits for them, and re-layouts  1.29 us (1%)
    pallas_call x1, Pallas kernels, shards(): pl.pallas_call(functools.partial(exchange_kernel, chunks), out_shape=(jax...  79.5 us
    pallas_call x1, Pallas kernels, shards(): pl.pallas_call(step_kernel, out_shape=jax.ShapeDtypeStruct(flat, f32), in...  17.2 us

profile of v1, /device:TPU:1, one launch (start us, length us, event | category | flops | bytes accessed | tf_op | source)
XLA Modules:
  0.0 98.6 jit_solution(16772630449213866814)
XLA Ops:
  0.0 0.6 pad_add_fusion.edge
  0.6 1.3 %copy.6.coupling = f32[2,5,5]{2,1,0:T(8,128)} copy(f32[2,5,5]{2,0,1:T(2,128)} %param.8) | data formatting | bytes 400 | tf_op args[3]
  1.9 79.5 %exchange.1 = (f32[20,5,48,128]{3,2,1,0:T(8,128)}, f32[10,5,48,128]{3,2,1,0:T(8,128)}) custom-call(s32[32]{0:T(128)} %clone.1, f32[2,10,32,512]{3,2,1,0:T(8,128)} %bitcast.6, f32[2,10,32,512]{3,2,1,0:T(8,128)} %bitcast.7, f32[10,32,512]{2,1,0:T(8,128)} %bitcast.8), custom_call_target="tpu_custom_call" | custom-call | tf_op jit(solution)/shard_map/exchange/pallas_call | solution.py:257
  81.4 17.2 %steps.1 = f32[2,10,32,512]{3,2,1,0:T(8,128)} custom-call(f32[2,5,5]{2,1,0:T(8,128)} %copy.6.coupling, s32[2]{0:T(128)} %pad_add_fusion.edge, f32[20,5,48,128]{3,2,1,0:T(8,128)} %get-tuple-element.7.e_ref, f32[10,5,48,128]{3,2,1,0:T(8,128)} %get-tuple-element.8.f_ref), custom_call_target="tpu_custom_call" | custom-call | tf_op jit(solution)/shard_map/steps/pallas_call | solution.py:282

commit v2 on v0

v2 whole, which is shorter than its diff:
```python
import functools

import jax
import jax.numpy as jnp
from jax import lax
from jax.experimental import pallas as pl
from jax.experimental.pallas import tpu as pltpu
from jax.sharding import PartitionSpec as P

HALO = 8
WIDE = 112
MESH = pl.DeviceIdType.MESH


def roll(values, shift):
    if isinstance(shift, int):
        shift = shift % 128
    return pltpu.roll(values, shift, axis=values.ndim - 1)


def kernel(
    nsrc, ndst, tab, clone, state, kick_hbm, forcing_hbm, coupling, out_ref,
    comb0, comb1, kick, forcing, picked, pool0, pool1, outgoing0, outgoing1,
    e0, e1, f_ref, work_a, work_b, pack0, pack1, packf, landed0, landed1, landedf, mix,
    load_sem, send1, recv1, send2, recv2, own_sem, edge_send, edge_recv,
):
    comb, pool, outgoing = (comb0, comb1), (pool0, pool1), (outgoing0, outgoing1)
    rim, pack, landed = (e0, e1), (pack0, pack1), (landed0, landed1)
    n = lax.axis_size("member")
    nlat = lax.axis_size("lat")
    me = lax.axis_index("member")
    lat = lax.axis_index("lat")
    across = 1 - lax.axis_index("lon")
    up = lax.rem(lat + nlat - 1, nlat)
    down = lax.rem(lat + 1, nlat)

    loads = [pltpu.make_async_copy(state.at[:, :, k], comb[k].at[0:2], load_sem.at[k]) for k in range(2)]
    loads.append(pltpu.make_async_copy(forcing_hbm, forcing, load_sem.at[2]))
    loads.append(pltpu.make_async_copy(kick_hbm, kick, load_sem.at[3]))
    for load in loads:
        load.start()

    barrier = pltpu.get_barrier_semaphore()

    def greet(r, _):
        pl.semaphore_signal(barrier, 1, device_id={"member": lax.rem(me + r, n)}, device_id_type=MESH)
        return 0

    lax.fori_loop(1, n, greet, 0)
    for peer in (
        {"lat": up}, {"lat": down}, {"lon": across},
        {"lat": up, "lon": across}, {"lat": down, "lon": across},
    ):
        pl.semaphore_signal(barrier, 1, device_id=peer, device_id_type=MESH)
    loads[0].wait()
    loads[1].wait()
    if nsrc == 1:
        first = tab[me] == 0

        def pick_one(v, c):
            for k in range(2):
                picked[0, v, k] = jnp.where(first, comb[k][0, v], comb[k][1, v])
            return c

        lax.fori_loop(0, 5, pick_one, 0)
    pl.semaphore_wait(barrier, n - 1 + 5)

    def window(piece):
        rows = pl.ds(pl.multiple_of(piece // 4 * 8, 8), 8)
        cols = pl.ds(pl.multiple_of(lax.rem(piece, 4) * 128, 128), 128)
        return rows, cols

    def given(k, rows, cols):
        if nsrc == 1:
            return picked.at[:, :, k, rows, cols]
        return comb[k].at[0:2, :, rows, cols]

    def spread(k, r):
        peer = lax.rem(me + r, n)
        return pltpu.make_async_remote_copy(
            given(k, *window(peer)), pool[k].at[me],
            send1.at[k, r], recv1.at[k, r], device_id={"member": peer}, device_id_type=MESH,
        )

    my_rows, my_cols = window(me)

    def collect(k, r):
        peer = lax.rem(me + r, n)
        return pltpu.make_async_remote_copy(
            outgoing[k].at[peer], comb[k].at[2 : 2 + ndst, :, my_rows, my_cols],
            send2.at[k, r], recv2.at[k, r], device_id={"member": peer}, device_id_type=MESH,
        )

    def peers(action):
        lax.fori_loop(1, n, lambda r, c: (action(r), c)[1], 0)

    for k in range(2):
        peers(lambda r: spread(k, r).start())
    owns = [pltpu.make_async_copy(given(k, my_rows, my_cols), pool[k].at[me], own_sem.at[k]) for k in range(2)]
    for own in owns:
        own.start()

    lane = lax.broadcasted_iota(jnp.int32, (32, 128), 1)

    def edge_copies(source, packed, arrived, base):
        hops = (
            (source.at[:, :, 8:16], source.at[:, :, 40:48], {"lat": up}),
            (source.at[:, :, 32:40], source.at[:, :, 0:8], {"lat": down}),
            (packed, arrived.at[:, 8:40], {"lon": across}),
            (packed.at[:, 0:8], arrived.at[:, 40:48], {"lat": up, "lon": across}),
            (packed.at[:, 24:32], arrived.at[:, 0:8], {"lat": down, "lon": across}),
        )
        return [
            pltpu.make_async_remote_copy(
                a, b, edge_send.at[base + i], edge_recv.at[base + i], device_id=peer, device_id_type=MESH
            )
            for i, (a, b, peer) in enumerate(hops)
        ]

    def lay_out(p, tiles, target, packed):
        target[p, 0, 8:40] = roll(tiles[0], 8)
        for c in range(1, 4):
            target[p, c, 8:40] = jnp.where(
                lane < 8 + 16 * c, roll(tiles[c - 1], 8 + 16 * c), roll(tiles[c], 8 + 16 * c)
            )
        target[p, 4, 8:40] = roll(tiles[3], 72)
        slot = lax.rem(p, 8)
        tile = roll(jnp.where(lane < 64, tiles[0], tiles[3]), 16 * slot)
        ours = lax.rem(lane + 8 + 128 - 16 * slot, 128) < 16
        packed[p // 8] = jnp.where(ours, tile, packed[p // 8])

    lane_tall = lax.broadcasted_iota(jnp.int32, (48, 128), 1)

    def add_columns(target, arrived):
        def one(p, c):
            turn = 128 - 16 * lax.rem(p, 8)
            source = arrived[p // 8]
            target[p, 0] = jnp.where(lane_tall < 8, roll(source, lax.rem(turn + 8, 128)), target[p, 0])
            target[p, 4] = jnp.where(lane_tall >= 72, roll(source, lax.rem(turn + 72, 128)), target[p, 4])
            return c

        lax.fori_loop(0, 10, one, 0)

    def clear_outside(target):
        @pl.when(lat == 0)
        def _():
            target[:, :, 0:8] = jnp.zeros((10, 5, 8, 128), jnp.float32)

        @pl.when(lat == nlat - 1)
        def _():
            target[:, :, 40:48] = jnp.zeros((10, 5, 8, 128), jnp.float32)

    def columns(ref, *index):
        return [ref[index + (slice(None), slice(t * 128, t * 128 + 128))] for t in range(4)]

    for k in range(2):
        pack[k][...] = jnp.zeros(pack[k].shape, jnp.float32)
    packf[...] = jnp.zeros(packf.shape, jnp.float32)
    loads[2].wait()

    def lay_forcing(p, c):
        tiles = columns(forcing, lax.rem(p, 5), p // 5)
        lay_out(p, [0.1 * t for t in tiles], f_ref, packf)
        return c

    lax.fori_loop(0, 10, lay_forcing, 0)
    f_copies = edge_copies(f_ref, packf, landedf, 10)
    for copy in f_copies:
        copy.start()

    for k in range(2):
        for v in range(5):
            table = coupling[v]
            for w in range(5):
                scaled = 0.25 * table[k, w]
                mix[k, v, w] = scaled + 0.75 if v == w else scaled

    for k in range(2):
        owns[k].wait()
        peers(lambda r: spread(k, r).wait_recv())

        def choose(d, c):
            for j in range(ndst):
                source = clone[2 * d + j] if ndst == 2 else clone[2 * d + tab[16 + d]]
                place = lax.rem(source, 2) if nsrc == 2 else 0
                outgoing[k][d, j] = pool[k][source // 2, place]
            return c

        lax.fori_loop(0, n, choose, 0)
        peers(lambda r: collect(k, r).start())
        mine = pltpu.make_async_copy(
            outgoing[k].at[me], comb[k].at[2 : 2 + ndst, :, my_rows, my_cols], own_sem.at[k]
        )
        mine.start()
        owns[k] = mine

    loads[3].wait()
    for k in range(2):
        peers(lambda r: spread(k, r).wait_send())
    for copy in f_copies:
        copy.wait()
    add_columns(f_ref, landedf)

    row_at = lax.broadcasted_iota(jnp.int32, (8, 128), 0)
    low = jnp.where(lat == 0, HALO, 0)
    high = jnp.where(lat == nlat - 1, 40, 48)
    near, far, first, second = 0.8 / 12.0, 0.05 / 12.0, 0.4 / 12.0, 0.05 / 12.0

    def sweep(k, source, target, starts):
        def tile(it, carry):
            m, c = it // 5, lax.rem(it, 5)
            for row in starts:
                centre = [source[5 * m + v, c, row : row + 8] for v in range(5)]
                u1, v1 = centre[0] * first, centre[1] * first
                u2, v2 = centre[0] * second, centre[1] * second
                ce1, cw1, ce2, cw2 = near - u1, near + u1, u2 - far, -far - u2
                cs1, cn1, cs2, cn2 = near - v1, near + v1, v2 - far, -far - v2
                for v in range(5):
                    p = 5 * m + v
                    here = centre[v]
                    along = cw1 * roll(here, 1) + ce1 * roll(here, -1)
                    along = along + (cw2 * roll(here, 2) + ce2 * roll(here, -2))
                    cross = cn1 * source[p, c, row - 1 : row + 7] + cs1 * source[p, c, row + 1 : row + 9]
                    cross = cross + (
                        cn2 * source[p, c, row - 2 : row + 6] + cs2 * source[p, c, row + 2 : row + 10]
                    )
                    rest = f_ref[5 * k + v, c, row : row + 8] + mix[k, v, 0] * centre[0]
                    for q in range(1, 5):
                        rest = rest + mix[k, v, q] * centre[q]
                    total = (along + cross) + rest
                    if row < 8 or row > 32:
                        inside = (row_at + row >= low) & (row_at + row < high)
                        total = jnp.where(inside, total, 0.0)
                    target[p, c, row : row + 8] = total
            return carry

        lax.fori_loop(0, 10, tile, 0)

    for k in range(2):
        owns[k].wait()
        peers(lambda r: collect(k, r).wait_recv())

        def begin(p, c):
            m, v = p // 5, lax.rem(p, 5)
            source = clone[2 * me + m]
            other = 2 + m if ndst == 2 else 2
            pick = jnp.where(source // 2 == me, lax.rem(source, 2), other)
            taken = columns(comb[k], pick, v)
            kicks = columns(kick, m, v, k)
            lay_out(p, [a + b for a, b in zip(taken, kicks)], rim[k], pack[k])
            return c

        lax.fori_loop(0, 10, begin, 0)
        copies = edge_copies(rim[k], pack[k], landed[k], 5 * k)
        for copy in copies:
            copy.start()
        for copy in copies:
            copy.wait()
        add_columns(rim[k], landed[k])
        clear_outside(rim[k])
        sweep(k, rim[k], work_a, (2, 10, 18, 26, 34, 38))
        sweep(k, work_a, work_b, (4, 12, 20, 28, 36))
        sweep(k, work_b, work_a, (6, 14, 22, 30, 34))
        sweep(k, work_a, work_b, (8, 16, 24, 32))

        def finish(p, c):
            m, v = p // 5, lax.rem(p, 5)
            turned = [roll(work_b[p, t, 8:40], -8 - 16 * t) for t in range(5)]
            for t in range(4):
                out_ref[m, v, k, :, t * 128 : t * 128 + 128] = jnp.where(
                    lane < WIDE - 16 * t, turned[t], turned[t + 1]
                )
            return c

        lax.fori_loop(0, 10, finish, 0)

    for k in range(2):
        peers(lambda r: collect(k, r).wait_send())


def run(nsrc, ndst, tab, clone_src, state, kick, forcing, coupling):
    n = lax.axis_size("member")
    f32 = jnp.float32
    vmem = pl.BlockSpec(memory_space=pltpu.VMEM)
    smem = pl.BlockSpec(memory_space=pltpu.SMEM)
    hbm = pl.BlockSpec(memory_space=pl.ANY)
    dma = pltpu.SemaphoreType.DMA
    member = state.shape[1:]
    level = (member[0],) + member[2:]
    padded = pltpu.VMEM((10, 5, 48, 128), f32)
    packed = pltpu.VMEM((2, 32, 128), f32)
    arrived = pltpu.VMEM((2, 48, 128), f32)
    return pl.pallas_call(
        functools.partial(kernel, nsrc, ndst),
        out_shape=jax.ShapeDtypeStruct(state.shape, f32),
        in_specs=[smem, smem, hbm, hbm, hbm, vmem],
        out_specs=vmem,
        scratch_shapes=[
            pltpu.VMEM((2 + ndst,) + level, f32), pltpu.VMEM((2 + ndst,) + level, f32),
            pltpu.VMEM(state.shape, f32), pltpu.VMEM(member, f32), pltpu.VMEM((1,) + member, f32),
            pltpu.VMEM((n, nsrc, 5, 8, 128), f32), pltpu.VMEM((n, nsrc, 5, 8, 128), f32),
            pltpu.VMEM((n, ndst, 5, 8, 128), f32), pltpu.VMEM((n, ndst, 5, 8, 128), f32),
            padded, padded, padded, padded, padded,
            packed, packed, packed, arrived, arrived, arrived,
            pltpu.SMEM((2, 5, 5), f32),
            dma((4,)), dma((2, n)), dma((2, n)), dma((2, n)), dma((2, n)),
            dma((2,)), dma((15,)), dma((15,)),
        ],
        compiler_params=pltpu.CompilerParams(collective_id=2 * nsrc + ndst, has_side_effects=True),
        name=f"advance_{nsrc}_{ndst}",
    )(tab, clone_src, state, kick, forcing, coupling.transpose(1, 0, 2))


def shards(state, kick, forcing, coupling, clone_src):
    return run(2, 2, clone_src, clone_src, state, kick, forcing, coupling)


def solution(mesh):
    block = P("member", None, None, "lat", "lon")
    in_specs = (block, block, P(None, None, "lat", "lon"), P(), P())
    return jax.shard_map(shards, mesh=mesh, in_specs=in_specs, out_specs=block, check_vma=False)
```

time: 358 us -> 93.8 us (0.26); the launches traced: 354 us -> 93.6 us
  waiting for transfers between devices: 255 us -> 0 us
  Pallas kernels: 0 us -> 91.1 us
  matrix products: 24.9 us -> 0 us
  starting transfers between devices: 22.4 us -> 0 us
  local copies, waits for them, and re-layouts: 20.8 us -> 2.51 us
  other arithmetic: 16.9 us -> 0 us
  between operations: 13.7 us -> 0.01 us
    all_gather x1 -> x0, waiting for transfers between devices: 232 us -> none  [shards(): piece = lax.all_gather(state, 'member', axis=0, tiled=True)]
    pallas_call x0 -> x1, Pallas kernels: none -> 91.1 us  [run(): pl.pallas_call(functools.partial(kernel, nsrc, ndst), out_shape=jax.Shape...]
    dot_general x4 -> x0, matrix products: 24.9 us -> none  [advance(): jnp.einsum('kvw,mwkij->mvkij', coupling, centre, precision=lax.Precision....]
    ppermute x16 -> x0, waiting for transfers between devices: 22.6 us -> none  [the longest x8 12.3 us: with_halo(): lax.ppermute(lax.slice_in_dim(block, 0, width, axis=dim), axis, backward)]
    ppermute x16 -> x0, starting transfers between devices: 22.4 us -> none  [the longest x8 12.3 us: with_halo(): lax.ppermute(lax.slice_in_dim(block, 0, width, axis=dim), axis, backward)]
    gather x1 -> x0, local copies, waits for them, and re-layouts: 7.59 us -> none  [shards(): rows = jnp.take(piece, jnp.clip(sources, 0, count - 1), axis=0)]
    select_n x4 -> x0, other arithmetic: 5.13 us -> none  [zero_rows(): return jnp.where(keep[:, None], values, 0.0)]
    ppermute x8 -> x0, local copies, waits for them, and re-layouts: 4.95 us -> none  [the longest x4 3.54 us: with_halo(): lax.ppermute(lax.slice_in_dim(block, 0, width, axis=dim), axis, backward)]
  transfers between devices with their start and end apart: 17 -> 0, of which waited for: 16 -> 0; matrix products, arithmetic and copies ran while one was open for 1% -> 0% of each run, Pallas kernels for 0% -> 0%
where the time goes in v2:
time: 93.8 us; the launch traced here: 93.6 us
  Pallas kernels  91.1 us (97%)
  local copies, waits for them, and re-layouts  2.51 us (3%)
    pallas_call x1, Pallas kernels, run(): pl.pallas_call(functools.partial(kernel, nsrc, ndst), out_shape=jax.Shape...  91.1 us
    unnamed x1, local copies, waits for them, and re-layouts  2.51 us

profile of v2, /device:TPU:1, one launch (start us, length us, event | category | flops | bytes accessed | tf_op | source)
XLA Modules:
  0.0 93.6 jit_solution(5212615865224275692)
XLA Ops:
  0.0 91.1 %advance_2_2.1 = f32[2,5,2,32,512]{4,3,2,1,0:T(8,128)} custom-call(s32[32]{0:T(128)} %clone.1, s32[32]{0:T(128)} %clone.1, f32[2,5,2,32,512]{4,3,2,1,0:T(8,128)} %state.1, f32[2,5,2,32,512]{4,3,2,1,0:T(8,128)} %kick_hbm.1, f32[5,2,32,512]{3,2,1,0:T(8,128)} %forcing_hbm.1, f32[5,2,5]{2,1,0:T(2,128)} %bitcast.1), custom_call_target="tpu_custom_call" | custom-call | tf_op jit(solution)/shard_map/advance_2_2/pallas_call | solution.py:293
  91.1 2.5 %copy.7 = f32[2,5,2,32,512]{4,3,2,1,0:T(8,128)} copy(f32[2,5,2,32,512]{4,3,2,1,0:T(8,128)} %advance_2_2.1) | data formatting | bytes 2621440

commit v3 on v2

--- a/solution.py
+++ b/solution.py
@@ -311,8 +311,51 @@
     )(tab, clone_src, state, kick, forcing, coupling.transpose(1, 0, 2))
 
 
+def plan_kernel(clone, tab, wanted):
+    def clear(m, c):
+        wanted[m] = 0
+        return c
+
+    lax.fori_loop(0, 32, clear, 0)
+
+    def mark(m, c):
+        source = clone[m]
+
+        @pl.when(jnp.right_shift(source, 1) != jnp.right_shift(m, 1))
+        def _():
+            wanted[source] = 1
+
+        return c
+
+    lax.fori_loop(0, 32, mark, 0)
+
+    def count(d, most):
+        gives, takes = most
+        tab[d] = jnp.where(wanted[2 * d] == 1, 0, 1)
+        gives = jnp.maximum(gives, wanted[2 * d] + wanted[2 * d + 1] - 1)
+        one, two = clone[2 * d], clone[2 * d + 1]
+        far_one = jnp.right_shift(one, 1) != d
+        far_two = jnp.right_shift(two, 1) != d
+        tab[16 + d] = jnp.where(far_one, 0, 1)
+        both = far_one & far_two & (one != two)
+        return gives, jnp.maximum(takes, jnp.where(both, 1, 0))
+
+    gives, takes = lax.fori_loop(0, 16, count, (jnp.int32(0), jnp.int32(0)))
+    tab[32] = 2 * gives + takes
+
+
 def shards(state, kick, forcing, coupling, clone_src):
-    return run(2, 2, clone_src, clone_src, state, kick, forcing, coupling)
+    smem = pl.BlockSpec(memory_space=pltpu.SMEM)
+    tab = pl.pallas_call(
+        plan_kernel,
+        out_shape=jax.ShapeDtypeStruct((33,), jnp.int32),
+        in_specs=[smem],
+        out_specs=smem,
+        scratch_shapes=[pltpu.SMEM((32,), jnp.int32)],
+        name="plan",
+    )(clone_src)
+    cases = [functools.partial(run, nsrc, ndst) for nsrc in (1, 2) for ndst in (1, 2)]
+    return lax.switch(tab[32], cases, tab, clone_src, state, kick, forcing, coupling)
 
 
 def solution(mesh):

time: 93.8 us -> 71.5 us (0.76)
  Pallas kernels: 91.1 us -> 68.7 us
    pallas_call x1, Pallas kernels: 91.1 us -> 66.8 us  [run(): pl.pallas_call(functools.partial(kernel, nsrc, ndst), out_shape=jax.Shape...]
    pallas_call x0 -> x1, Pallas kernels: none -> 1.93 us  [shards(): pl.pallas_call(plan_kernel, out_shape=jax.ShapeDtypeStruct((33,), jnp.int...]
    unnamed x1, local copies, waits for them, and re-layouts: 2.51 us -> 1.06 us
where the time goes in v3:
time: 71.5 us; the launch traced here: 71 us
  Pallas kernels  68.7 us (96%)
  local copies, waits for them, and re-layouts  1.64 us (2%)
    pallas_call x1, Pallas kernels, run(): pl.pallas_call(functools.partial(kernel, nsrc, ndst), out_shape=jax.Shape...  66.8 us
    pallas_call x1, Pallas kernels, shards(): pl.pallas_call(plan_kernel, out_shape=jax.ShapeDtypeStruct((33,), jnp.int...  1.93 us

profile of v3, /device:TPU:1, one launch (start us, length us, event | category | flops | bytes accessed | tf_op | source)
XLA Modules:
  0.0 71.0 jit_solution(15189985428692398585)
XLA Ops:
  0.0 1.9 %plan.1 = s32[33]{0:T(128)S(1)} custom-call(s32[32]{0:T(128)} %clone.1), custom_call_target="tpu_custom_call" | custom-call | tf_op jit(solution)/shard_map/plan/pallas_call | solution.py:349
  1.9 0.6 slice.3
  3.2 66.8 %conditional.1 = (f32[2,5,2,32,512]{4,3,2,1,0:T(8,128)S(1)}) conditional(s32[]{:T(128)} %bitcast.4, (f32[2,5,5]{2,0,1:T(2,128)}, s32[33]{0:T(128)S(1)}, s32[32]{0:T(128)}, f32[2,5,2,32,512]{4,3,2,1,0:T(8,128)}, f32[2,5,2,32,512]{4,3,2,1,0:T(8,128)}, /*index=5*/f32[5,2,32,512]{3,2,1,0:T(8,128)}) %tuple.17, ...), branch_computations={%region_0.0_spmd, %region_1.0_spmd, %region_2.0_spmd, %region_3.0_... | conditional | bytes 8 | solution.py:358
  3.2 66.8 %advance_1_1.1 = f32[2,5,2,32,512]{4,3,2,1,0:T(8,128)S(1)} custom-call(s32[33]{0:T(128)S(1)} %get-tuple-element.56.tab, s32[32]{0:T(128)} %get-tuple-element.58.clone, f32[2,5,2,32,512]{4,3,2,1,0:T(8,128)} %get-tuple-element.60.state, f32[2,5,2,32,512]{4,3,2,1,0:T(8,128)} %get-tuple-element.61.kick_hbm, f32[5,2,32,512]{3,2,1,0:T(8,128)} %get-tuple-element.62.forcing_hbm, ...), custom_call_target="tpu_custom_call" | custom-call | tf_op jit(solution)/shard_map/cond/branch_0_fun/advance_1_1/pallas_call | solution.py:293
  70.0 1.1 %copy.15 = f32[2,5,2,32,512]{4,3,2,1,0:T(8,128)} copy(f32[2,5,2,32,512]{4,3,2,1,0:T(8,128)S(1)} %get-tuple-element.82) | data formatting | bytes 2621440

commit v4 on v3

--- a/solution.py
+++ b/solution.py
@@ -21,7 +21,7 @@
 def kernel(
     nsrc, ndst, tab, clone, state, kick_hbm, forcing_hbm, coupling, out_ref,
     comb0, comb1, kick, forcing, picked, pool0, pool1, outgoing0, outgoing1,
-    e0, e1, f_ref, work_a, work_b, pack0, pack1, packf, landed0, landed1, landedf, mix,
+    e0, e1, f_ref, work_a, work_b, pack0, pack1, packf, landed0, landed1, landedf, mix, shift,
     load_sem, send1, recv1, send2, recv2, own_sem, edge_send, edge_recv,
 ):
     comb, pool, outgoing = (comb0, comb1), (pool0, pool1), (outgoing0, outgoing1)
@@ -175,6 +175,15 @@
                 scaled = 0.25 * table[k, w]
                 mix[k, v, w] = scaled + 0.75 if v == w else scaled
 
+    row_in = lax.broadcasted_iota(jnp.int32, (256, 256), 0)
+    col_out = lax.broadcasted_iota(jnp.int32, (256, 256), 1)
+    step = jnp.bitwise_and(row_in - col_out + 256, 127)
+    one, two = jnp.where(step == 1, 1.0, 0.0), jnp.where(step == 2, 1.0, 0.0)
+    back_one, back_two = jnp.where(step == 127, 1.0, 0.0), jnp.where(step == 126, 1.0, 0.0)
+    slope = 8.0 * (one - back_one) - (two - back_two)
+    spread_out = 16.0 * (one + back_one) - (two + back_two)
+    shift[...] = jnp.where(col_out < 128, slope, spread_out).astype(jnp.bfloat16)
+
     for k in range(2):
         owns[k].wait()
         peers(lambda r: spread(k, r).wait_recv())
@@ -209,17 +218,23 @@
     def sweep(k, source, target, starts):
         def tile(it, carry):
             m, c = it // 5, lax.rem(it, 5)
-            for row in starts:
+            field = jnp.concatenate(
+                [source[5 * m + v, c, row : row + 8] for row in starts for v in range(5)], axis=0
+            )
+            coarse = field.astype(jnp.bfloat16)
+            fine = (field - coarse.astype(jnp.float32)).astype(jnp.bfloat16)
+            lonwise = jnp.dot(
+                jnp.concatenate([coarse, fine], axis=1), shift[...], preferred_element_type=jnp.float32
+            )
+            for i, row in enumerate(starts):
                 centre = [source[5 * m + v, c, row : row + 8] for v in range(5)]
-                u1, v1 = centre[0] * first, centre[1] * first
-                u2, v2 = centre[0] * second, centre[1] * second
-                ce1, cw1, ce2, cw2 = near - u1, near + u1, u2 - far, -far - u2
+                u2 = centre[0] * second
+                v1, v2 = centre[1] * first, centre[1] * second
                 cs1, cn1, cs2, cn2 = near - v1, near + v1, v2 - far, -far - v2
                 for v in range(5):
                     p = 5 * m + v
-                    here = centre[v]
-                    along = cw1 * roll(here, 1) + ce1 * roll(here, -1)
-                    along = along + (cw2 * roll(here, 2) + ce2 * roll(here, -2))
+                    at = 8 * (5 * i + v)
+                    along = far * lonwise[at : at + 8, 128:256] - u2 * lonwise[at : at + 8, 0:128]
                     cross = cn1 * source[p, c, row - 1 : row + 7] + cs1 * source[p, c, row + 1 : row + 9]
                     cross = cross + (
                         cn2 * source[p, c, row - 2 : row + 6] + cs2 * source[p, c, row + 2 : row + 10]
@@ -302,7 +317,7 @@
             pltpu.VMEM((n, ndst, 5, 8, 128), f32), pltpu.VMEM((n, ndst, 5, 8, 128), f32),
             padded, padded, padded, padded, padded,
             packed, packed, packed, arrived, arrived, arrived,
-            pltpu.SMEM((2, 5, 5), f32),
+            pltpu.SMEM((2, 5, 5), f32), pltpu.VMEM((256, 256), jnp.bfloat16),
             dma((4,)), dma((2, n)), dma((2, n)), dma((2, n)), dma((2, n)),
             dma((2,)), dma((15,)), dma((15,)),
         ],

time: 71.5 us -> 95.2 us (1.33)
  Pallas kernels: 68.7 us -> 92.7 us
    pallas_call x1, Pallas kernels: 66.8 us -> 90.8 us  [run(): pl.pallas_call(functools.partial(kernel, nsrc, ndst), out_shape=jax.Shape...]
where the time goes in v4:
time: 95.2 us; the launch traced here: 95.1 us
  Pallas kernels  92.7 us (97%)
  local copies, waits for them, and re-layouts  1.64 us (2%)
    pallas_call x1, Pallas kernels, run(): pl.pallas_call(functools.partial(kernel, nsrc, ndst), out_shape=jax.Shape...  90.8 us
    pallas_call x1, Pallas kernels, shards(): pl.pallas_call(plan_kernel, out_shape=jax.ShapeDtypeStruct((33,), jnp.int...  1.93 us

profile of v4, /device:TPU:1, one launch (start us, length us, event | category | flops | bytes accessed | tf_op | source)
XLA Modules:
  0.0 95.1 jit_solution(13229937359806314662)
XLA Ops:
  0.0 1.9 %plan.1 = s32[33]{0:T(128)S(1)} custom-call(s32[32]{0:T(128)} %clone.1), custom_call_target="tpu_custom_call" | custom-call | tf_op jit(solution)/shard_map/plan/pallas_call | solution.py:364
  1.9 0.6 slice.3
  3.2 90.8 %conditional.1 = (f32[2,5,2,32,512]{4,3,2,1,0:T(8,128)S(1)}) conditional(s32[]{:T(128)} %bitcast.4, (f32[2,5,5]{2,0,1:T(2,128)}, s32[33]{0:T(128)S(1)}, s32[32]{0:T(128)}, f32[2,5,2,32,512]{4,3,2,1,0:T(8,128)}, f32[2,5,2,32,512]{4,3,2,1,0:T(8,128)}, /*index=5*/f32[5,2,32,512]{3,2,1,0:T(8,128)}) %tuple.17, ...), branch_computations={%region_0.0_spmd, %region_1.0_spmd, %region_2.0_spmd, %region_3.0_... | conditional | bytes 8 | solution.py:373
  3.2 90.8 %advance_2_2.1 = f32[2,5,2,32,512]{4,3,2,1,0:T(8,128)S(1)} custom-call(s32[33]{0:T(128)S(1)} %get-tuple-element.76.tab, s32[32]{0:T(128)} %get-tuple-element.77.clone, f32[2,5,2,32,512]{4,3,2,1,0:T(8,128)} %get-tuple-element.78.state, f32[2,5,2,32,512]{4,3,2,1,0:T(8,128)} %get-tuple-element.79.kick_hbm, f32[5,2,32,512]{3,2,1,0:T(8,128)} %get-tuple-element.80.forcing_hbm, ...), custom_call_target="tpu_custom_call" | custom-call | tf_op jit(solution)/shard_map/cond/branch_3_fun/advance_2_2/pallas_call | solution.py:308
  94.0 1.1 %copy.15 = f32[2,5,2,32,512]{4,3,2,1,0:T(8,128)} copy(f32[2,5,2,32,512]{4,3,2,1,0:T(8,128)S(1)} %get-tuple-element.82) | data formatting | bytes 2621440
